TPU v7x, 32 devices: a whole 2x2x4 slice. The times are simulated.
32 devices in a mesh: dp: 8 (over y, x, core), tensor: 4 (over z).
Axes of the slice: x: 2, y: 2, z: 4, core: 2. Of those that a mesh axis runs over, the one named last changes fastest.
Arguments:
- tokens: bfloat16 [8, 1024, 1280], P('dp', 'tensor'), may hold values from -6 to 6
- lengths: int32 [8], P('dp'), may hold values from 256 to 1024, as said below
- cotangent: bfloat16 [8, 1024, 1280], P('dp', 'tensor'), may hold values from -6 to 6
- ln1_gain: bfloat16 [1280], P('dp'), may hold values from 0.099609375 to 1.8984375
- ln1_bias: bfloat16 [1280], P('dp'), may hold values from -3 to 3
- query_weight: bfloat16 [1280, 1280], P('dp', 'tensor'), may hold values from -0.25 to 0.25
- query_bias: bfloat16 [1280], P('tensor'), may hold values from -3 to 3
- key_weight: bfloat16 [1280, 1280], P('dp', 'tensor'), may hold values from -0.25 to 0.25
- value_weight: bfloat16 [1280, 1280], P('dp', 'tensor'), may hold values from -0.15625 to 0.15625
- value_bias: bfloat16 [1280], P('tensor'), may hold values from -3 to 3
- out_weight: bfloat16 [1280, 1280], P('dp', 'tensor'), may hold values from -1.25 to 1.25
- out_bias: bfloat16 [1280], P('dp'), may hold values from -3 to 3
- ln2_gain: bfloat16 [1280], P('dp'), may hold values from 0.099609375 to 1.8984375
- ln2_bias: bfloat16 [1280], P('dp'), may hold values from -3 to 3
- up_weight: bfloat16 [1280, 5120], P('dp', 'tensor'), may hold values from -0.15625 to 0.15625
- up_bias: bfloat16 [5120], P('tensor'), may hold values from -3 to 3
- down_weight: bfloat16 [1280, 5120], P('dp', 'tensor'), may hold values from -0.25 to 0.25
- down_bias: bfloat16 [1280], P('dp'), may hold values from -3 to 3
Outputs:
- output: bfloat16 [8, 1024, 1280], P('dp', 'tensor')
- tokens_grad: float32 [8, 1024, 1280], P('dp', 'tensor')
- ln1_gain_grad: float32 [1280], P('dp')
- ln1_bias_grad: float32 [1280], P('dp')
- query_weight_grad: float32 [1280, 1280], P('dp', 'tensor')
- query_bias_grad: float32 [1280], P('tensor')
- key_weight_grad: float32 [1280, 1280], P('dp', 'tensor')
- value_weight_grad: float32 [1280, 1280], P('dp', 'tensor')
- value_bias_grad: float32 [1280], P('tensor')
- out_weight_grad: float32 [1280, 1280], P('dp', 'tensor')
- out_bias_grad: float32 [1280], P('dp')
- ln2_gain_grad: float32 [1280], P('dp')
- ln2_bias_grad: float32 [1280], P('dp')
- up_weight_grad: float32 [1280, 5120], P('dp', 'tensor')
- up_bias_grad: float32 [5120], P('tensor')
- down_weight_grad: float32 [1280, 5120], P('dp', 'tensor')
- down_bias_grad: float32 [1280], P('dp')
Inputs may be any that keep to these rules, and one draw needn't show every extreme that they name: `lengths`: positions of a clip at or past its length are padding and are masked as keys; some clip has exactly 1024 valid positions and some exactly 256.
All inputs are finite; a program needn't handle non-finite values.
Results may differ from a plain program's by a relative error of at most 0.02.
Values may be sent and summed in bfloat16 or wider, within the bound.
No kernel may reach another device: no remote copies, remote signals or barrier semaphores. Data moves between devices by JAX's collectives and lax.ppermute only.
A program may use at most 128 MiB of HBM per device.

v0:
```python
import jax
import jax.numpy as jnp
from jax import lax
from jax.sharding import PartitionSpec as P

HEAD_DIM = 80
masked_score = -1e30


def layer_norm(values, gain, shift):
    centre = values - jnp.mean(values, axis=-1, keepdims=True)
    spread = jnp.mean(centre * centre, axis=-1, keepdims=True)
    return centre * lax.rsqrt(spread + 1e-05) * gain + shift


def masked_scores(query_part, key_rows, length, scale):
    seq = key_rows.shape[0]
    valid = lax.broadcasted_iota(jnp.int32, (seq,), 0) < length
    scores = (
        jnp.einsum("qhe,khe->hqk", query_part, key_rows, preferred_element_type=jnp.float32) * scale
    )
    return jnp.where(valid[None, None, :], scores, masked_score)


def attend_clip(query_rows, key_rows, value_rows, length, blocks):
    seq, heads = (query_rows.shape[0], query_rows.shape[1])
    scale = HEAD_DIM ** (-0.5)
    query_blocks = query_rows.reshape(blocks, seq // blocks, heads, HEAD_DIM)

    def one_block(query_part):
        scores = masked_scores(query_part, key_rows, length, scale)
        top = jnp.max(scores, axis=-1, keepdims=True)
        expo = jnp.exp(scores - top)
        total = jnp.sum(expo, axis=-1, keepdims=True)
        probs = (expo / total).astype(jnp.bfloat16)
        context = jnp.einsum(
            "hqk,khe->qhe", probs, value_rows, preferred_element_type=jnp.float32
        ).astype(jnp.bfloat16)
        return (context, (top + jnp.log(total))[..., 0])

    context, log_total = lax.map(one_block, query_blocks)
    return (context.reshape(seq, heads, HEAD_DIM), log_total)


def attend_back(query_rows, key_rows, value_rows, context_grad, log_total, length, blocks):
    seq, heads = (query_rows.shape[0], query_rows.shape[1])
    scale = HEAD_DIM ** (-0.5)
    query_blocks = query_rows.reshape(blocks, seq // blocks, heads, HEAD_DIM)
    grad_blocks = context_grad.reshape(blocks, seq // blocks, heads, HEAD_DIM)

    def one_block(carry, inputs):
        key_acc, value_acc = carry
        query_part, grad_part, lse_part = inputs
        scores = masked_scores(query_part, key_rows, length, scale)
        probs = jnp.exp(scores - lse_part[..., None])
        value_acc = value_acc + jnp.einsum(
            "hqk,qhe->khe",
            probs.astype(jnp.bfloat16),
            grad_part,
            preferred_element_type=jnp.float32,
        )
        prob_grad = jnp.einsum(
            "qhe,khe->hqk", grad_part, value_rows, preferred_element_type=jnp.float32
        )
        centred = prob_grad - jnp.sum(probs * prob_grad, axis=-1, keepdims=True)
        score_grad = (probs * centred).astype(jnp.bfloat16)
        query_grad = (
            jnp.einsum("hqk,khe->qhe", score_grad, key_rows, preferred_element_type=jnp.float32)
            * scale
        )
        key_acc = (
            key_acc
            + jnp.einsum("hqk,qhe->khe", score_grad, query_part, preferred_element_type=jnp.float32)
            * scale
        )
        return ((key_acc, value_acc), query_grad.astype(jnp.bfloat16))

    zeros = jnp.zeros((seq, heads, HEAD_DIM), jnp.float32)
    (key_acc, value_acc), query_grad = lax.scan(
        one_block, (zeros, zeros), (query_blocks, grad_blocks, log_total)
    )
    return (
        query_grad.reshape(seq, heads, HEAD_DIM),
        key_acc.astype(jnp.bfloat16),
        value_acc.astype(jnp.bfloat16),
    )


def forward_pass(tokens, lengths, weights):
    (
        ln1_gain,
        ln1_bias,
        query_weight,
        query_bias,
        key_weight,
        value_weight,
        value_bias,
        out_weight,
        out_bias,
        ln2_gain,
        ln2_bias,
        up_weight,
        up_bias,
        down_weight,
        down_bias,
    ) = weights
    query_full, key_full, value_full, out_full, gain_one, bias_one, out_shift = (
        lax.all_gather(query_weight, "dp", axis=0, tiled=True),
        lax.all_gather(key_weight, "dp", axis=0, tiled=True),
        lax.all_gather(value_weight, "dp", axis=0, tiled=True),
        lax.all_gather(out_weight, "dp", axis=0, tiled=True),
        lax.all_gather(ln1_gain, "dp", axis=0, tiled=True),
        lax.all_gather(ln1_bias, "dp", axis=0, tiled=True),
        lax.all_gather(out_bias, "dp", axis=0, tiled=True),
    )
    gain_one = gain_one.astype(jnp.float32)
    bias_one = bias_one.astype(jnp.float32)
    rows = tokens.astype(jnp.float32)
    normed = layer_norm(rows, gain_one, bias_one).astype(jnp.bfloat16)
    normed_all = lax.all_gather(normed, "tensor", axis=1, tiled=True)
    clips, seq = (normed_all.shape[0], normed_all.shape[1])
    heads = query_full.shape[1] // HEAD_DIM
    blocks = seq // 512
    shaped = (clips, seq, heads, HEAD_DIM)
    queries = (
        (
            jnp.einsum("csd,dh->csh", normed_all, query_full, preferred_element_type=jnp.float32)
            + query_bias.astype(jnp.float32)
        )
        .astype(jnp.bfloat16)
        .reshape(shaped)
    )
    keyed = (
        jnp.einsum("csd,dh->csh", normed_all, key_full, preferred_element_type=jnp.float32)
        .astype(jnp.bfloat16)
        .reshape(shaped)
    )
    valued = (
        (
            jnp.einsum("csd,dh->csh", normed_all, value_full, preferred_element_type=jnp.float32)
            + value_bias.astype(jnp.float32)
        )
        .astype(jnp.bfloat16)
        .reshape(shaped)
    )

    def clip_attend(item):
        return attend_clip(item[0], item[1], item[2], item[3], blocks)

    context, log_total = lax.map(clip_attend, (queries, keyed, valued, lengths))
    context = context.reshape(clips, seq, heads * HEAD_DIM)
    attn_terms = jnp.einsum("csh,dh->csd", context, out_full, preferred_element_type=jnp.float32)
    attended = lax.psum_scatter(
        attn_terms.astype(jnp.bfloat16), "tensor", scatter_dimension=1, tiled=True
    ).astype(jnp.float32)
    middle = rows + attended + out_shift.astype(jnp.float32)
    up_full, down_full, gain_two, bias_two, down_shift = (
        lax.all_gather(up_weight, "dp", axis=0, tiled=True),
        lax.all_gather(down_weight, "dp", axis=0, tiled=True),
        lax.all_gather(ln2_gain, "dp", axis=0, tiled=True),
        lax.all_gather(ln2_bias, "dp", axis=0, tiled=True),
        lax.all_gather(down_bias, "dp", axis=0, tiled=True),
    )
    gain_two = gain_two.astype(jnp.float32)
    bias_two = bias_two.astype(jnp.float32)
    normed_two = layer_norm(middle, gain_two, bias_two).astype(jnp.bfloat16)
    normed_two_all = lax.all_gather(normed_two, "tensor", axis=1, tiled=True)
    hidden_pre = jnp.einsum(
        "csd,df->csf", normed_two_all, up_full, preferred_element_type=jnp.float32
    ) + up_bias.astype(jnp.float32)
    hidden = jax.nn.gelu(hidden_pre, approximate=False).astype(jnp.bfloat16)
    mlp_terms = jnp.einsum("csf,df->csd", hidden, down_full, preferred_element_type=jnp.float32)
    mixed = lax.psum_scatter(
        mlp_terms.astype(jnp.bfloat16), "tensor", scatter_dimension=1, tiled=True
    ).astype(jnp.float32)
    output = middle + mixed + down_shift.astype(jnp.float32)
    return {
        "output": output,
        "rows": rows,
        "normed_all": normed_all,
        "queries": queries,
        "keyed": keyed,
        "valued": valued,
        "context": context,
        "log_total": log_total,
        "middle": middle,
        "normed_two_all": normed_two_all,
        "hidden_pre": hidden_pre,
        "hidden": hidden,
        "query_full": query_full,
        "key_full": key_full,
        "value_full": value_full,
        "out_full": out_full,
        "up_full": up_full,
        "down_full": down_full,
        "gain_one": gain_one,
        "bias_one": bias_one,
        "gain_two": gain_two,
        "bias_two": bias_two,
        "blocks": blocks,
    }


def local(
    tokens,
    lengths,
    cotangent,
    ln1_gain,
    ln1_bias,
    query_weight,
    query_bias,
    key_weight,
    value_weight,
    value_bias,
    out_weight,
    out_bias,
    ln2_gain,
    ln2_bias,
    up_weight,
    up_bias,
    down_weight,
    down_bias,
):
    weights = (
        ln1_gain,
        ln1_bias,
        query_weight,
        query_bias,
        key_weight,
        value_weight,
        value_bias,
        out_weight,
        out_bias,
        ln2_gain,
        ln2_bias,
        up_weight,
        up_bias,
        down_weight,
        down_bias,
    )
    first = forward_pass(tokens, lengths, weights)
    fenced_tokens, fenced_lengths, fenced_weights, fenced_output = lax.optimization_barrier(
        (tokens, lengths, weights, first["output"])
    )
    saved = forward_pass(fenced_tokens, fenced_lengths, fenced_weights)
    blocks = saved["blocks"]
    grad_out = cotangent.astype(jnp.float32)
    down_shift_grad = jnp.sum(grad_out, axis=(0, 1))
    grad_out_all = lax.all_gather(cotangent, "tensor", axis=1, tiled=True)
    down_grad = jnp.einsum(
        "csd,csf->df", grad_out_all, saved["hidden"], preferred_element_type=jnp.float32
    )
    hidden_grad = jnp.einsum(
        "csd,df->csf", grad_out_all, saved["down_full"], preferred_element_type=jnp.float32
    )
    gelu_pull = jax.vjp(lambda pre: jax.nn.gelu(pre, approximate=False), saved["hidden_pre"])[1]
    pre_grad = gelu_pull(hidden_grad)[0].astype(jnp.bfloat16)
    up_shift_grad = jnp.sum(pre_grad, axis=(0, 1), dtype=jnp.float32)
    up_grad = jnp.einsum(
        "csd,csf->df", saved["normed_two_all"], pre_grad, preferred_element_type=jnp.float32
    )
    up_grad_shard, down_grad_shard = (
        lax.psum_scatter(
            up_grad.astype(jnp.bfloat16), "dp", scatter_dimension=0, tiled=True
        ).astype(jnp.float32),
        lax.psum_scatter(
            down_grad.astype(jnp.bfloat16), "dp", scatter_dimension=0, tiled=True
        ).astype(jnp.float32),
    )
    normed_two_terms = jnp.einsum(
        "csf,df->csd", pre_grad, saved["up_full"], preferred_element_type=jnp.float32
    )
    normed_two_grad = lax.psum_scatter(
        normed_two_terms.astype(jnp.bfloat16), "tensor", scatter_dimension=1, tiled=True
    ).astype(jnp.float32)
    norm_pull = jax.vjp(layer_norm, saved["middle"], saved["gain_two"], saved["bias_two"])[1]
    middle_part, gain_two_grad, bias_two_grad = norm_pull(normed_two_grad)
    middle_grad = grad_out + middle_part
    out_shift_grad = jnp.sum(middle_grad, axis=(0, 1))
    middle_all = lax.all_gather(middle_grad.astype(jnp.bfloat16), "tensor", axis=1, tiled=True)
    out_grad = jnp.einsum(
        "csd,csh->dh", middle_all, saved["context"], preferred_element_type=jnp.float32
    )
    context_grad = jnp.einsum(
        "csd,dh->csh", middle_all, saved["out_full"], preferred_element_type=jnp.float32
    ).astype(jnp.bfloat16)
    queries = saved["queries"]
    clips, seq, heads = (queries.shape[0], queries.shape[1], queries.shape[2])

    def clip_back(item):
        return attend_back(item[0], item[1], item[2], item[3], item[4], item[5], blocks)

    query_grad, key_grad, value_grad = lax.map(
        clip_back,
        (
            queries,
            saved["keyed"],
            saved["valued"],
            context_grad.reshape(clips, seq, heads, HEAD_DIM),
            saved["log_total"],
            lengths,
        ),
    )
    flat = (clips, seq, heads * HEAD_DIM)
    query_grad = query_grad.reshape(flat)
    key_grad = key_grad.reshape(flat)
    value_grad = value_grad.reshape(flat)
    normed_all = saved["normed_all"]
    query_weight_grad = jnp.einsum(
        "csd,csh->dh", normed_all, query_grad, preferred_element_type=jnp.float32
    )
    key_weight_grad = jnp.einsum(
        "csd,csh->dh", normed_all, key_grad, preferred_element_type=jnp.float32
    )
    value_weight_grad = jnp.einsum(
        "csd,csh->dh", normed_all, value_grad, preferred_element_type=jnp.float32
    )
    query_shift_grad = jnp.sum(query_grad, axis=(0, 1), dtype=jnp.float32)
    value_shift_grad = jnp.sum(value_grad, axis=(0, 1), dtype=jnp.float32)
    normed_terms = (
        jnp.einsum(
            "csh,dh->csd", query_grad, saved["query_full"], preferred_element_type=jnp.float32
        )
        + jnp.einsum("csh,dh->csd", key_grad, saved["key_full"], preferred_element_type=jnp.float32)
        + jnp.einsum(
            "csh,dh->csd", value_grad, saved["value_full"], preferred_element_type=jnp.float32
        )
    )
    normed_grad = lax.psum_scatter(
        normed_terms.astype(jnp.bfloat16), "tensor", scatter_dimension=1, tiled=True
    ).astype(jnp.float32)
    first_pull = jax.vjp(layer_norm, saved["rows"], saved["gain_one"], saved["bias_one"])[1]
    tokens_part, gain_one_grad, bias_one_grad = first_pull(normed_grad)
    tokens_grad = middle_grad + tokens_part
    summed = lax.psum(
        (
            gain_one_grad,
            bias_one_grad,
            out_shift_grad,
            gain_two_grad,
            bias_two_grad,
            down_shift_grad,
        ),
        "tensor",
    )
    owned = (
        lax.psum_scatter(
            query_weight_grad.astype(jnp.bfloat16), "dp", scatter_dimension=0, tiled=True
        ).astype(jnp.float32),
        lax.psum_scatter(
            key_weight_grad.astype(jnp.bfloat16), "dp", scatter_dimension=0, tiled=True
        ).astype(jnp.float32),
        lax.psum_scatter(
            value_weight_grad.astype(jnp.bfloat16), "dp", scatter_dimension=0, tiled=True
        ).astype(jnp.float32),
        lax.psum_scatter(
            out_grad.astype(jnp.bfloat16), "dp", scatter_dimension=0, tiled=True
        ).astype(jnp.float32),
        lax.psum_scatter(
            summed[0].astype(jnp.bfloat16), "dp", scatter_dimension=0, tiled=True
        ).astype(jnp.float32),
        lax.psum_scatter(
            summed[1].astype(jnp.bfloat16), "dp", scatter_dimension=0, tiled=True
        ).astype(jnp.float32),
        lax.psum_scatter(
            summed[2].astype(jnp.bfloat16), "dp", scatter_dimension=0, tiled=True
        ).astype(jnp.float32),
        lax.psum_scatter(
            summed[3].astype(jnp.bfloat16), "dp", scatter_dimension=0, tiled=True
        ).astype(jnp.float32),
        lax.psum_scatter(
            summed[4].astype(jnp.bfloat16), "dp", scatter_dimension=0, tiled=True
        ).astype(jnp.float32),
        lax.psum_scatter(
            summed[5].astype(jnp.bfloat16), "dp", scatter_dimension=0, tiled=True
        ).astype(jnp.float32),
    )
    shared = lax.psum((query_shift_grad, value_shift_grad, up_shift_grad), "dp")
    return (
        first["output"].astype(jnp.bfloat16),
        tokens_grad,
        owned[4],
        owned[5],
        owned[0],
        shared[0],
        owned[1],
        owned[2],
        shared[1],
        owned[3],
        owned[6],
        owned[7],
        owned[8],
        up_grad_shard,
        shared[2],
        down_grad_shard,
        owned[9],
    )


def solution(mesh):
    placed = (
        P("dp", "tensor", None),
        P("dp"),
        P("dp", "tensor", None),
        P("dp"),
        P("dp"),
        P("dp", "tensor"),
        P("tensor"),
        P("dp", "tensor"),
        P("dp", "tensor"),
        P("tensor"),
        P("dp", "tensor"),
        P("dp"),
        P("dp"),
        P("dp"),
        P("dp", "tensor"),
        P("tensor"),
        P("dp", "tensor"),
        P("dp"),
    )
    return jax.shard_map(
        local,
        mesh=mesh,
        in_specs=placed,
        out_specs=(
            P("dp", "tensor", None),
            P("dp", "tensor", None),
            P("dp"),
            P("dp"),
            P("dp", "tensor"),
            P("tensor"),
            P("dp", "tensor"),
            P("dp", "tensor"),
            P("tensor"),
            P("dp", "tensor"),
            P("dp"),
            P("dp"),
            P("dp"),
            P("dp", "tensor"),
            P("tensor"),
            P("dp", "tensor"),
            P("dp"),
        ),
        check_vma=False,
    )
```

profile of v0, /device:TPU:0, one launch (start us, length us, event | category | flops | bytes accessed | tf_op | source)
XLA Modules:
  0.0 1138.2 jit_solution(9833556908998333741)
XLA Ops:
  15.2 25.5 %all-reduce.21 = (bf16[1280]{0:T(1024)(128)(2,1)S(1)}, bf16[1280]{0:T(1024)(128)(2,1)S(1)}, bf16[1280]{0:T(1024)(128)(2,1)S(1)}, bf16[1280]{0:T(1024)(128)(2,1)S...) all-reduce(bf16[1280]{0:T(1024)(128)(2,1)S(1)} %dynamic-update-slic, ...), channel_id=1, replica_groups=mesh['dp'=8,'tensor'=4] {'dp'}, use_global_device_ids=true, to_apply=%add.1 | all-reduce | flops 7680 | bytes 30720
  45.8 10.9 all_gather.90
  56.7 11.0 all_gather.92
  67.8 11.6 %all_gather.91 = bf16[1280,320]{1,0:T(8,128)(2,1)} all-gather(bf16[160,320]{1,0:T(8,128)(2,1)S(1)} %copy-done.25), channel_id=1, replica_groups=mesh['dp'=8,'tensor'=4] {'dp'}, dimensions={0}, use_global_device_ids=true | all-gather | bytes 921600 | tf_op jit(solution)/shard_map/all_gather | solution.py:109
  109.7 25.4 %while.64 = (s32[]{:T(128)}, bf16[2,512,4,80]{1,3,2,0:T(8,128)(2,1)S(1)}, s32[]{:T(128)}, bf16[2,512,4,80]{1,3,2,0:T(8,128)(2,1)S(1)}, bf16[1024,4,80]{0,2,1:T(8...) while((s32[]{:T(128)}, bf16[2,512,4,80]{1,3,2,0:T(8,128)(2,1)S(1)}, s32[]{:T(128)}, ...), condition=%wide.region_5.6_spmd, body=%wide.region_2.5_spmd.sunk | while | flops 683837440 | bytes 21383284 | solution.py:41
  140.3 49.8 %reduce-scatter.14.cloned.1.call-done = bf16[1,256,1280]{2,1,0:T(8,128)(2,1)} async-done(((bf16[1,1024,1280]{2,1,0:T(8,128)(2,1)}), bf16[1,256,1280]{2,1,0:T(8,128)(2,1)}) %reduce-scatter.14.cloned.1.call-update) | async-done | bytes 655376 | tf_op jit(solution)/shard_map/reduce_scatter | solution.py:153
  195.8 11.6 %all-gather.17.cloned.1.call-done = bf16[1280,1280]{1,0:T(8,128)(2,1)} async-done(((bf16[160,1280]{1,0:T(8,128)(2,1)}), bf16[1280,1280]{1,0:T(8,128)(2,1)}) %all-gather.17.cloned.1.call-update) | async-done | bytes 3276816 | tf_op jit(solution)/shard_map/all_gather | solution.py:159
  207.3 56.7 %all-gather.13.cloned.1.call-done = bf16[1,1024,1280]{2,1,0:T(8,128)(2,1)} async-done(((bf16[1,256,1280]{2,1,0:T(8,128)(2,1)}), bf16[1,1024,1280]{2,1,0:T(8,128)(2,1)}) %all-gather.13.cloned.1.call-update) | async-done | bytes 2621456 | tf_op jit(solution)/shard_map/all_gather | solution.py:167
  264.0 21.3 %fusion.96 = bf16[1,1024,1280]{2,1,0:T(8,128)(2,1)} fusion(bf16[1280,1280]{1,0:T(8,128)(2,1)} %all-gather.17.cloned.1.call-done, bf16[1280,1280]{1,0:T(8,128)(2,1)} %all-gather.15.cloned.1.call-done, bf16[1,1024,1280]{2,1,0:T(8,128)(2,1)} %all-gather.13.cloned.1.call-done, f32[1280]{0:T(1024)S(1)} %convert_element_type.308), kind=kOutput, calls=%fused_computation.127 | convolution fusion | flops 6798704640 | bytes 11801600 | tf_op jit(solution)/shard_map/csf,df->csd/dot_general | solution.py:172
  285.5 50.9 %reduce-scatter.16.cloned.1.call-done = bf16[1,256,1280]{2,1,0:T(8,128)(2,1)} async-done(((bf16[1,1024,1280]{2,1,0:T(8,128)(2,1)}), bf16[1,256,1280]{2,1,0:T(8,128)(2,1)}) %reduce-scatter.16.cloned.1.call-update) | async-done | bytes 655376 | tf_op jit(solution)/shard_map/reduce_scatter | solution.py:173
  340.5 23.8 %all-reduce.20 = (bf16[1280]{0:T(1024)(128)(2,1)S(1)}, bf16[1280]{0:T(1024)(128)(2,1)S(1)}, bf16[1280]{0:T(1024)(128)(2,1)S(1)}, bf16[1280]{0:T(1024)(128)(2,1)S(1)}, bf16[1280]{0:T(1024)(128)(2,1)S(1)}) all-reduce(bf16[1280]{0:T(1024)(128)(2,1)S(1)} %dynamic-update-slice.10, ...), channel_id=1, replica_groups=mesh['dp'=8,'tensor'=4] {'dp'}, use_global_device_ids=true, to_apply=%add.10 | all-reduce | flops 6400 | bytes 25600
  365.6 10.9 all_gather.106
  376.5 11.0 all_gather.105
  397.8 12.1 %all_gather.107 = bf16[1280,320]{1,0:T(8,128)(2,1)} all-gather(bf16[160,320]{1,0:T(8,128)(2,1)S(1)} %copy-done.29), channel_id=1, replica_groups=mesh['dp'=8,'tensor'=4] {'dp'}, dimensions={0}, use_global_device_ids=true | all-gather | bytes 921600 | tf_op jit(solution)/shard_map/all_gather | solution.py:111
  430.5 13.7 %while.65 = (s32[]{:T(128)}, bf16[2,512,4,80]{1,3,2,0:T(8,128)(2,1)S(1)}, f32[2,4,512]{2,1,0:T(4,128)S(1)}, s32[]{:T(128)}, bf16[2,512,4,80]{1,3,2,0:T(8,128)(2,...) while((s32[]{:T(128)}, ...), condition=%wide.region_15.16_spmd, body=%wide.region_12.15_spmd.sunk | while | flops 696417280 | bytes 27201636 | solution.py:41
  451.0 50.2 %reduce-scatter.18.cloned.1.call-done = bf16[1,256,1280]{2,1,0:T(8,128)(2,1)} async-done(((bf16[1,1024,1280]{2,1,0:T(8,128)(2,1)}), bf16[1,256,1280]{2,1,0:T(8,128)(2,1)}) %reduce-scatter.18.cloned.1.call-update) | async-done | bytes 655376 | tf_op jit(solution)/shard_map/reduce_scatter | solution.py:153
  507.6 27.8 %all-gather.23.cloned.1.call-done = bf16[1280,1280]{1,0:T(8,128)(2,1)} async-done(((bf16[160,1280]{1,0:T(8,128)(2,1)}), bf16[1280,1280]{1,0:T(8,128)(2,1)}) %all-gather.23.cloned.1.call-update) | async-done | bytes 3276816 | tf_op jit(solution)/shard_map/all_gather | solution.py:158
  535.4 56.8 %all-gather.21.cloned.1.call-done = bf16[1,1024,1280]{2,1,0:T(8,128)(2,1)} async-done(((bf16[1,256,1280]{2,1,0:T(8,128)(2,1)}), bf16[1,1024,1280]{2,1,0:T(8,128)(2,1)}) %all-gather.21.cloned.1.call-update) | async-done | bytes 2621456 | tf_op jit(solution)/shard_map/all_gather | solution.py:167
  592.3 17.6 %fusion.75 = (f32[1024,1280]{1,0:T(8,128)}, f32[1024,1280]{1,0:T(8,128)}) fusion(f32[1280]{0:T(1024)S(1)} %convert_element_type.332, bf16[1280,1280]{1,0:T(8,128)(2,1)} %all-gather.23.cloned.1.call-done, bf16[1,1024,1280]{2,1,0:T(8,128)(2,1)} %all-gather.21.cloned.1.call-done), kind=kOutput, calls=%fused_computation.81 | convolution fusion | flops 3438018560 | bytes 16389120 | tf_op jit(solution)/shard_map/csd,df->csf/dot_general | solution.py:168
  609.9 37.3 %all-gather.27.cloned.1.call-done = bf16[1,1024,1280]{2,1,0:T(8,128)(2,1)} async-done(((bf16[1,256,1280]{2,1,0:T(8,128)(2,1)}), bf16[1,1024,1280]{2,1,0:T(8,128)(2,1)}) %all-gather.27.cloned.1.call-update) | async-done | bytes 2621456 | tf_op jit(solution)/shard_map/all_gather | solution.py:249
  647.1 33.2 %all-gather.25.cloned.1.call-done = bf16[1280,1280]{1,0:T(8,128)(2,1)} async-done(((bf16[160,1280]{1,0:T(8,128)(2,1)}), bf16[1280,1280]{1,0:T(8,128)(2,1)}) %all-gather.25.cloned.1.call-update) | async-done | bytes 3276816 | tf_op jit(solution)/shard_map/all_gather | solution.py:159
  680.4 11.4 convert_reduce_fusion
  698.2 52.2 %reduce-scatter.20.cloned.1.call-done = bf16[1,256,1280]{2,1,0:T(8,128)(2,1)} async-done(((bf16[1,1024,1280]{2,1,0:T(8,128)(2,1)}), bf16[1,256,1280]{2,1,0:T(8,128)(2,1)}) %reduce-scatter.20.cloned.1.call-update) | async-done | bytes 655376 | tf_op jit(solution)/shard_map/reduce_scatter | solution.py:273
  783.2 30.0 %all-gather.29.cloned.1.call-done = bf16[1,1024,1280]{2,1,0:T(8,128)(2,1)} async-done(((bf16[1,256,1280]{2,1,0:T(8,128)(2,1)}), bf16[1,1024,1280]{2,1,0:T(8,128)(2,1)}) %all-gather.29.cloned.1.call-update) | async-done | bytes 2621456 | tf_op jit(solution)/shard_map/all_gather | solution.py:280
  823.2 41.3 %while.66 = (s32[]{:T(128)}, f32[1024,4,80]{0,2,1:T(8,128)S(1)}, f32[1024,4,80]{0,2,1:T(8,128)}, bf16[2,512,4,80]{1,3,2,0:T(8,128)(2,1)}, bf16[2,512,4,80]{1,3,2...) while((s32[]{:T(128)}, f32[1024,4,80]{0,2,1:T(8,128)S(1)}, ...), condition=%wide.region_24.25_spmd.clone, body=%wide.region_22.24_spmd.clone.sunk | while | flops 1711143936 | bytes 144175888 | solution.py:79
  899.7 24.7 %all-reduce.17 = (f32[320]{0:T(512)}, f32[320]{0:T(512)}, f32[1280]{0:T(1024)}) all-reduce(f32[320]{0:T(512)S(1)} %reduce_sum.247, f32[320]{0:T(512)S(1)} %reduce_sum.249, f32[1280]{0:T(1024)S(1)} %copy-done.43), channel_id=1, replica_groups=mesh['dp'=8,'tensor'=4] {'dp'}, use_global_device_ids=true, to_apply=%region_36.37 | all-reduce | flops 1920 | bytes 15360 | tf_op jit(solution)/shard_map/psum | solution.py:378
  926.0 23.7 %reduce-scatter.26.cloned.1.call-done = bf16[160,320]{1,0:T(8,128)(2,1)} async-done(((bf16[1280,320]{1,0:T(8,128)(2,1)}), bf16[160,320]{1,0:T(8,128)(2,1)}) %reduce-scatter.26.cloned.1.call-update) | async-done | bytes 102416 | tf_op jit(solution)/shard_map/reduce_scatter | solution.py:350
  951.2 37.2 %reduce-scatter.30.cloned.1.call-done = bf16[160,320]{1,0:T(8,128)(2,1)} async-done(((bf16[1280,320]{1,0:T(8,128)(2,1)}), bf16[160,320]{1,0:T(8,128)(2,1)}) %reduce-scatter.30.cloned.1.call-update) | async-done | bytes 102416 | tf_op jit(solution)/shard_map/reduce_scatter | solution.py:356
  990.1 37.6 %reduce-scatter.24.cloned.1.call-done = bf16[160,320]{1,0:T(8,128)(2,1)} async-done(((bf16[1280,320]{1,0:T(8,128)(2,1)}), bf16[160,320]{1,0:T(8,128)(2,1)}) %reduce-scatter.24.cloned.1.call-update) | async-done | bytes 102416 | tf_op jit(solution)/shard_map/reduce_scatter | solution.py:347
  1029.3 52.9 %reduce-scatter.22.cloned.1.call-done = bf16[1,256,1280]{2,1,0:T(8,128)(2,1)} async-done(((bf16[1,1024,1280]{2,1,0:T(8,128)(2,1)}), bf16[1,256,1280]{2,1,0:T(8,128)(2,1)}) %reduce-scatter.22.cloned.1.call-update) | async-done | bytes 655376 | tf_op jit(solution)/shard_map/reduce_scatter | solution.py:329
  1085.6 17.8 %all-reduce.18 = (bf16[1280]{0:T(1024)(128)(2,1)S(1)}, bf16[1280]{0:T(1024)(128)(2,1)S(1)}, bf16[1280]{0:T(1024)(128)(2,1)S(1)}, bf16[1280]{0:T(1024)(128)(2,1)S...) all-reduce(f32[1280]{0:T(1024)S(1)} %get-tuple-element.403, ...), channel_id=1, replica_groups=mesh['dp'=8,'tensor'=4] {'tensor'}, use_global_device_ids=true, to_apply=%region_29.30 | all-reduce | flops 7680 | bytes 46080 | tf_op jit(solution)/shard_map/psum | solution.py:335
  1103.3 22.4 %all-reduce.19 = (bf16[1280]{0:T(1024)(128)(2,1)S(1)}, bf16[1280]{0:T(1024)(128)(2,1)S(1)}, bf16[1280]{0:T(1024)(128)(2,1)S(1)}, bf16[1280]{0:T(1024)(128)(2,1)S...) all-reduce(bf16[1280]{0:T(1024)(128)(2,1)S(1)} %get-tuple-element.4, ...), channel_id=7, replica_groups=mesh['dp'=8,'tensor'=4] {'dp'}, use_global_device_ids=true, to_apply=%region_30.31.clone | all-reduce | flops 7680 | bytes 30720
  (333 shorter events, 279.6 us)
Async XLA Ops:
  8.1 92.0 %all-gather.11.cloned.1.call-start = ((), (), s32[]{:S(2)}) async-start(), calls=%async_computation.11 | async-start | bytes 3276800 | tf_op jit(solution)/shard_map/all_gather | solution.py:120
  45.7 144.3 %reduce-scatter.14.cloned.1.call-start = ((), (), s32[]{:S(2)}) async-start(), calls=%async_computation.12 | async-start | bytes 3276800 | tf_op jit(solution)/shard_map/reduce_scatter | solution.py:153
  139.0 56.7 %all-gather.15.cloned.1.call-start = ((), (), s32[]{:S(2)}) async-start(), calls=%async_computation.14 | async-start | bytes 3686400 | tf_op jit(solution)/shard_map/all_gather | solution.py:158
  139.6 67.7 %all-gather.17.cloned.1.call-start = ((), (), s32[]{:S(2)}) async-start(), calls=%async_computation.15 | async-start | bytes 3686400 | tf_op jit(solution)/shard_map/all_gather | solution.py:159
  140.2 123.8 %all-gather.13.cloned.1.call-start = ((), (), s32[]{:S(2)}) async-start(), calls=%async_computation.13 | async-start | bytes 3276800 | tf_op jit(solution)/shard_map/all_gather | solution.py:167
  195.3 141.2 %reduce-scatter.16.cloned.1.call-start = ((), (), s32[]{:S(2)}) async-start(), calls=%async_computation.16 | async-start | bytes 3276800 | tf_op jit(solution)/shard_map/reduce_scatter | solution.py:173
  195.7 140.7 %copy-start.9 = (bf16[1,256,1280]{2,1,0:T(8,128)(2,1)S(1)}, bf16[1,256,1280]{2,1,0:T(8,128)(2,1)}, u32[]{:S(2)}) copy-start(bf16[1,256,1280]{2,1,0:T(8,128)(2,1)} %reduce-scatter.14.cloned.1.call-done) | copy-start | bytes 1966084
  285.4 133.1 %all-gather.19.cloned.1.call-start = ((), (), s32[]{:S(2)}) async-start(), calls=%async_computation.17 | async-start | bytes 3276800 | tf_op jit(solution)/shard_map/all_gather | solution.py:120
  365.5 135.7 %reduce-scatter.18.cloned.1.call-start = ((), (), s32[]{:S(2)}) async-start(), calls=%async_computation.18 | async-start | bytes 3276800 | tf_op jit(solution)/shard_map/reduce_scatter | solution.py:153
  450.2 85.2 %all-gather.23.cloned.1.call-start = ((), (), s32[]{:S(2)}) async-start(), calls=%async_computation.20 | async-start | bytes 3686400 | tf_op jit(solution)/shard_map/all_gather | solution.py:158
  451.0 141.3 %all-gather.21.cloned.1.call-start = ((), (), s32[]{:S(2)}) async-start(), calls=%async_computation.19 | async-start | bytes 3276800 | tf_op jit(solution)/shard_map/all_gather | solution.py:167
  506.4 140.7 %all-gather.27.cloned.1.call-start = ((), (), s32[]{:S(2)}) async-start(), calls=%async_computation.22 | async-start | bytes 3276800 | tf_op jit(solution)/shard_map/all_gather | solution.py:249
  507.0 173.4 %all-gather.25.cloned.1.call-start = ((), (), s32[]{:S(2)}) async-start(), calls=%async_computation.21 | async-start | bytes 3686400 | tf_op jit(solution)/shard_map/all_gather | solution.py:159
  507.6 242.8 %reduce-scatter.20.cloned.1.call-start = ((), (), s32[]{:S(2)}) async-start(), calls=%async_computation.23 | async-start | bytes 3276800 | tf_op jit(solution)/shard_map/reduce_scatter | solution.py:273
  698.2 115.0 %all-gather.29.cloned.1.call-start = ((), (), s32[]{:S(2)}) async-start(), calls=%async_computation.24 | async-start | bytes 3276800 | tf_op jit(solution)/shard_map/all_gather | solution.py:280
  758.6 135.2 %reduce-scatter.34.cloned.1.call-start = ((), (), s32[]{:S(2)}) async-start(), calls=%async_computation.31 | async-start | bytes 3686400
  774.9 121.3 %reduce-scatter.32.cloned.1.call-start = ((), (), s32[]{:S(2)}) async-start(), calls=%async_computation.30 | async-start | bytes 3686400 | tf_op jit(solution)/shard_map/reduce_scatter | solution.py:263
  782.9 141.4 %reduce-scatter.28.cloned.1.call-start = ((), (), s32[]{:S(2)}) async-start(), calls=%async_computation.28 | async-start | bytes 1105920 | tf_op jit(solution)/shard_map/reduce_scatter | solution.py:353
  871.1 78.6 %reduce-scatter.26.cloned.1.call-start = ((), (), s32[]{:S(2)}) async-start(), calls=%async_computation.27 | async-start | bytes 1105920 | tf_op jit(solution)/shard_map/reduce_scatter | solution.py:350
  875.8 112.6 %reduce-scatter.30.cloned.1.call-start = ((), (), s32[]{:S(2)}) async-start(), calls=%async_computation.29 | async-start | bytes 1105920 | tf_op jit(solution)/shard_map/reduce_scatter | solution.py:356
  880.2 147.5 %reduce-scatter.24.cloned.1.call-start = ((), (), s32[]{:S(2)}) async-start(), calls=%async_computation.26 | async-start | bytes 1105920 | tf_op jit(solution)/shard_map/reduce_scatter | solution.py:347
  886.5 195.6 %reduce-scatter.22.cloned.1.call-start = ((), (), s32[]{:S(2)}) async-start(), calls=%async_computation.25 | async-start | bytes 3276800 | tf_op jit(solution)/shard_map/reduce_scatter | solution.py:329
  893.0 189.2 %copy-start.3 = (bf16[1,256,1280]{2,1,0:T(8,128)(2,1)S(1)}, bf16[1,256,1280]{2,1,0:T(8,128)(2,1)}, u32[]{:S(2)}) copy-start(bf16[1,256,1280]{2,1,0:T(8,128)(2,1)} %param.24) | copy-start | bytes 1966084
  893.0 189.2 %copy-start.31 = (f32[1280]{0:T(1024)S(1)}, f32[1280]{0:T(1024)}, u32[]{:S(2)}) copy-start(f32[1280]{0:T(1024)} %copy-done.30) | copy-start | bytes 15364
  893.0 189.2 %copy-start.33 = (f32[256]{0:T(256)S(1)}, f32[256]{0:T(256)}, u32[]{:S(2)}) copy-start(f32[256]{0:T(256)} %copy-done.32) | copy-start | bytes 3076
  895.0 188.7 %copy-start.42 = (f32[256]{0:T(256)S(1)}, f32[256]{0:T(256)}, u32[]{:S(2)}) copy-start(f32[256]{0:T(256)} %copy-done.41) | copy-start | bytes 3076
  895.0 188.7 %copy-start.40 = (f32[256]{0:T(256)S(1)}, f32[256]{0:T(256)}, u32[]{:S(2)}) copy-start(f32[256]{0:T(256)} %copy-done.39) | copy-start | bytes 3076
  896.1 189.4 %copy-start.34 = (f32[1280]{0:T(1024)S(1)}, f32[1280]{0:T(1024)}, u32[]{:S(2)}) copy-start(f32[1280]{0:T(1024)} %get-tuple-element.405) | copy-start | bytes 15364
  896.1 189.4 %copy-start.35 = (f32[1280]{0:T(1024)S(1)}, f32[1280]{0:T(1024)}, u32[]{:S(2)}) copy-start(f32[1280]{0:T(1024)} %get-tuple-element.401) | copy-start | bytes 15364
  896.1 189.4 %copy-start.36 = (f32[1280]{0:T(1024)S(1)}, f32[1280]{0:T(1024)}, u32[]{:S(2)}) copy-start(f32[1280]{0:T(1024)} %get-tuple-element.483) | copy-start | bytes 15364
  896.1 189.4 %copy-start.37 = (f32[1280]{0:T(1024)S(1)}, f32[1280]{0:T(1024)}, u32[]{:S(2)}) copy-start(f32[1280]{0:T(1024)} %get-tuple-element.491) | copy-start | bytes 15364
  896.1 231.6 %copy-start.8 = (f32[1,256,1280]{2,1,0:T(8,128)S(1)}, f32[1,256,1280]{2,1,0:T(8,128)}, u32[]{:S(2)}) copy-start(f32[1,256,1280]{2,1,0:T(8,128)} %copy-done.7) | copy-start | bytes 3932164
  (52 other events, 1320.1 us)
Sparse Core Ops, SparseCore 0:
  45.8 54.1 all-gather.10
  139.1 50.8 reduce-scatter.13
  285.5 50.8 reduce-scatter.15
  365.6 52.9 all-gather.18
  698.3 52.0 reduce-scatter.19
  758.7 54.4 all-gather.28
Sparse Core Ops, SparseCore 1:
  141.4 31.4 all-gather.14
  174.6 32.7 all-gather.16
  209.4 54.6 all-gather.12
  450.3 50.9 reduce-scatter.17
  503.1 32.2 all-gather.22
  537.6 54.6 all-gather.20
  593.7 53.4 all-gather.26
  648.9 31.4 all-gather.24
  775.0 46.4 reduce-scatter.33
  824.8 46.7 reduce-scatter.31
  874.7 35.6 reduce-scatter.27
  913.9 35.6 reduce-scatter.25
  952.7 35.7 reduce-scatter.29
  992.0 35.6 reduce-scatter.23
  1030.0 52.1 reduce-scatter.21
where the time goes:
time: 1140 us
  waiting for transfers between devices  629 us (55%)
  blocking collectives  203 us (18%)
  matrix products  190 us (17%)
  other arithmetic  61 us (5%)
  local copies, waits for them, and re-layouts  34.6 us (3%)
  between operations  18.4 us (2%)
    all_gather x2, waiting for transfers between devices, forward_pass(): normed_two_all = lax.all_gather(normed_two, 'tensor', axis=1, tiled=True)  114 us
    reduce_scatter x2, waiting for transfers between devices, forward_pass(): lax.psum_scatter(attn_terms.astype(jnp.bfloat16), 'tensor', scatter_dimen...  99.9 us
    unnamed x3, blocking collectives  71.7 us
    reduce_scatter x1, waiting for transfers between devices, local(): lax.psum_scatter(normed_terms.astype(jnp.bfloat16), 'tensor', scatter_dim...  52.9 us
    reduce_scatter x1, waiting for transfers between devices, local(): lax.psum_scatter(normed_two_terms.astype(jnp.bfloat16), 'tensor', scatter...  52.2 us
    reduce_scatter x1, waiting for transfers between devices, forward_pass(): lax.psum_scatter(mlp_terms.astype(jnp.bfloat16), 'tensor', scatter_dimens...  50.9 us
    all_gather x2, waiting for transfers between devices, forward_pass(): lax.all_gather(down_weight, 'dp', axis=0, tiled=True)  44.8 us
    reduce_scatter x1, waiting for transfers between devices, local(): lax.psum_scatter(query_weight_grad.astype(jnp.bfloat16), 'dp', scatter_di...  37.6 us
  transfers between devices with their start and end apart: 21, of which 17 were waited for; matrix products, arithmetic and copies ran while one was open for 12% of the time, Pallas kernels for 0%

commit v1 on v0

--- a/solution.py
+++ b/solution.py
@@ -5,6 +5,18 @@
 
 HEAD_DIM = 80
 masked_score = -1e30
+
+
+def push_things_on(x_in, along_axis):
+    n_dev_all = lax.axis_size(along_axis)
+    block_out = [(ii - 1, ii) for ii in range(1, n_dev_all)] + [(n_dev_all - 1, 0)]
+    mat_out = x_in
+    history = [mat_out]
+    for _ in range(n_dev_all - 1):
+        mat_out = lax.ppermute(mat_out, axis_name=along_axis, perm=block_out)
+        history += [mat_out]
+    right_arr = jnp.concatenate([*reversed(history)], axis=1)
+    return jnp.roll(right_arr, (lax.axis_index(along_axis) + 1) * mat_out.shape[1], axis=1)
 
 
 def layer_norm(values, gain, shift):
@@ -246,7 +258,7 @@
     blocks = saved["blocks"]
     grad_out = cotangent.astype(jnp.float32)
     down_shift_grad = jnp.sum(grad_out, axis=(0, 1))
-    grad_out_all = lax.all_gather(cotangent, "tensor", axis=1, tiled=True)
+    grad_out_all = push_things_on(cotangent, "tensor")
     down_grad = jnp.einsum(
         "csd,csf->df", grad_out_all, saved["hidden"], preferred_element_type=jnp.float32
     )

time: 1140 us -> 1090 us (0.956)
  waiting for transfers between devices: 629 us -> 571 us
    ppermute x0 -> x3, waiting for transfers between devices: none -> 62.3 us  [push_things_on(): mat_out = lax.ppermute(mat_out, axis_name=along_axis, perm=block_out)]
    all_gather x1 -> x0, waiting for transfers between devices: 37.3 us -> none  [local(): grad_out_all = lax.all_gather(cotangent, 'tensor', axis=1, tiled=True)]
    all_gather x2, waiting for transfers between devices: 114 us -> 76.4 us  [forward_pass(): normed_two_all = lax.all_gather(normed_two, 'tensor', axis=1, tiled=True)]
    all_gather x2, waiting for transfers between devices: 27.8 us -> 0.03 us  [forward_pass(): lax.all_gather(up_weight, 'dp', axis=0, tiled=True)]
    all_gather x2, waiting for transfers between devices: 44.8 us -> 26.6 us  [forward_pass(): lax.all_gather(down_weight, 'dp', axis=0, tiled=True)]
    unnamed x136 -> x134, local copies, waits for them, and re-layouts: 22.4 us -> 25 us
  transfers between devices with their start and end apart: 21 -> 23, of which waited for: 17 -> 18; matrix products, arithmetic and copies ran while one was open for 12% -> 14% of each run, Pallas kernels for 0% -> 0%
where the time goes in v1:
time: 1090 us
  waiting for transfers between devices  571 us (52%)
  blocking collectives  203 us (19%)
  matrix products  188 us (17%)
  other arithmetic  64.1 us (6%)
  local copies, waits for them, and re-layouts  38.1 us (3%)
  between operations  18.4 us (2%)
    reduce_scatter x2, waiting for transfers between devices, forward_pass(): lax.psum_scatter(attn_terms.astype(jnp.bfloat16), 'tensor', scatter_dimen...  99.9 us
    all_gather x2, waiting for transfers between devices, forward_pass(): normed_two_all = lax.all_gather(normed_two, 'tensor', axis=1, tiled=True)  76.4 us
    unnamed x3, blocking collectives  71.7 us
    ppermute x3, waiting for transfers between devices, push_things_on(): mat_out = lax.ppermute(mat_out, axis_name=along_axis, perm=block_out)  62.3 us
    reduce_scatter x1, waiting for transfers between devices, local(): lax.psum_scatter(normed_terms.astype(jnp.bfloat16), 'tensor', scatter_dim...  52.9 us
    reduce_scatter x1, waiting for transfers between devices, local(): lax.psum_scatter(normed_two_terms.astype(jnp.bfloat16), 'tensor', scatter...  52.2 us
    reduce_scatter x1, waiting for transfers between devices, forward_pass(): lax.psum_scatter(mlp_terms.astype(jnp.bfloat16), 'tensor', scatter_dimens...  50.9 us
    reduce_scatter x1, waiting for transfers between devices, local(): lax.psum_scatter(query_weight_grad.astype(jnp.bfloat16), 'dp', scatter_di...  37.5 us
  transfers between devices with their start and end apart: 23, of which 18 were waited for; matrix products, arithmetic and copies ran while one was open for 14% of the time, Pallas kernels for 0%

profile of v1, /device:TPU:0, one launch (start us, length us, event | category | flops | bytes accessed | tf_op | source)
XLA Modules:
  0.0 1085.7 jit_solution(14582369504636904582)
XLA Ops:
  15.2 25.5 %all-reduce.21 = (bf16[1280]{0:T(1024)(128)(2,1)S(1)}, bf16[1280]{0:T(1024)(128)(2,1)S(1)}, bf16[1280]{0:T(1024)(128)(2,1)S(1)}, bf16[1280]{0:T(1024)(128)(2,1)S...) all-reduce(bf16[1280]{0:T(1024)(128)(2,1)S(1)} %dynamic-update-slic, ...), channel_id=1, replica_groups=mesh['dp'=8,'tensor'=4] {'dp'}, use_global_device_ids=true, to_apply=%add.1 | all-reduce | flops 7680 | bytes 30720
  47.1 12.1 %all_gather.87 = bf16[1280,320]{1,0:T(8,128)(2,1)} all-gather(bf16[160,320]{1,0:T(8,128)(2,1)} %param.29), channel_id=1, replica_groups=mesh['dp'=8,'tensor'=4] {'dp'}, dimensions={0}, use_global_device_ids=true | all-gather | bytes 921600 | tf_op jit(solution)/shard_map/all_gather | solution.py:120
  69.3 12.0 %all_gather.88 = bf16[1280,320]{1,0:T(8,128)(2,1)} all-gather(bf16[160,320]{1,0:T(8,128)(2,1)S(1)} %copy-done.25), channel_id=1, replica_groups=mesh['dp'=8,'tensor'=4] {'dp'}, dimensions={0}, use_global_device_ids=true | all-gather | bytes 921600 | tf_op jit(solution)/shard_map/all_gather | solution.py:121
  81.3 11.0 %all_gather.90 = bf16[1280,320]{1,0:T(8,128)(2,1)S(1)} all-gather(bf16[160,320]{1,0:T(8,128)(2,1)S(1)} %copy-done.27), channel_id=1, replica_groups=mesh['dp'=8,'tensor'=4] {'dp'}, dimensions={0}, use_global_device_ids=true | all-gather | bytes 921600 | tf_op jit(solution)/shard_map/all_gather | solution.py:123
  109.6 25.3 %while.64 = (s32[]{:T(128)}, bf16[2,512,4,80]{1,3,2,0:T(8,128)(2,1)S(1)}, s32[]{:T(128)}, bf16[2,512,4,80]{1,3,2,0:T(8,128)(2,1)S(1)}, bf16[1024,4,80]{0,2,1:T(8...) while((s32[]{:T(128)}, bf16[2,512,4,80]{1,3,2,0:T(8,128)(2,1)S(1)}, s32[]{:T(128)}, ...), condition=%wide.region_5.6_spmd, body=%wide.region_2.5_spmd.sunk | while | flops 683837440 | bytes 21383284 | solution.py:53
  140.2 49.8 %reduce-scatter.12.cloned.1.call-done = bf16[1,256,1280]{2,1,0:T(8,128)(2,1)} async-done(((bf16[1,1024,1280]{2,1,0:T(8,128)(2,1)}), bf16[1,256,1280]{2,1,0:T(8,128)(2,1)}) %reduce-scatter.12.cloned.1.call-update) | async-done | bytes 655376 | tf_op jit(solution)/shard_map/reduce_scatter | solution.py:165
  195.7 11.6 %all-gather.16.cloned.1.call-done = bf16[1280,1280]{1,0:T(8,128)(2,1)} async-done(((bf16[160,1280]{1,0:T(8,128)(2,1)}), bf16[1280,1280]{1,0:T(8,128)(2,1)}) %all-gather.16.cloned.1.call-update) | async-done | bytes 3276816 | tf_op jit(solution)/shard_map/all_gather | solution.py:171
  207.2 56.7 %all-gather.12.cloned.1.call-done = bf16[1,1024,1280]{2,1,0:T(8,128)(2,1)} async-done(((bf16[1,256,1280]{2,1,0:T(8,128)(2,1)}), bf16[1,1024,1280]{2,1,0:T(8,128)(2,1)}) %all-gather.12.cloned.1.call-update) | async-done | bytes 2621456 | tf_op jit(solution)/shard_map/all_gather | solution.py:179
  263.9 21.3 %fusion.88 = bf16[1,1024,1280]{2,1,0:T(8,128)(2,1)} fusion(bf16[1280,1280]{1,0:T(8,128)(2,1)} %all-gather.16.cloned.1.call-done, bf16[1280,1280]{1,0:T(8,128)(2,1)} %all-gather.14.cloned.1.call-done, bf16[1,1024,1280]{2,1,0:T(8,128)(2,1)} %all-gather.12.cloned.1.call-done, f32[1280]{0:T(1024)S(1)} %convert_element_type.305), kind=kOutput, calls=%fused_computation.118 | convolution fusion | flops 6798704640 | bytes 11801600 | tf_op jit(solution)/shard_map/csf,df->csd/dot_general | solution.py:184
  285.4 50.9 %reduce-scatter.14.cloned.1.call-done = bf16[1,256,1280]{2,1,0:T(8,128)(2,1)} async-done(((bf16[1,1024,1280]{2,1,0:T(8,128)(2,1)}), bf16[1,256,1280]{2,1,0:T(8,128)(2,1)}) %reduce-scatter.14.cloned.1.call-update) | async-done | bytes 655376 | tf_op jit(solution)/shard_map/reduce_scatter | solution.py:185
  340.5 23.8 %all-reduce.20 = (bf16[1280]{0:T(1024)(128)(2,1)S(1)}, bf16[1280]{0:T(1024)(128)(2,1)S(1)}, bf16[1280]{0:T(1024)(128)(2,1)S(1)}, bf16[1280]{0:T(1024)(128)(2,1)S(1)}, bf16[1280]{0:T(1024)(128)(2,1)S(1)}) all-reduce(bf16[1280]{0:T(1024)(128)(2,1)S(1)} %dynamic-update-slice.10, ...), channel_id=1, replica_groups=mesh['dp'=8,'tensor'=4] {'dp'}, use_global_device_ids=true, to_apply=%add.10 | all-reduce | flops 6400 | bytes 25600
  376.4 11.0 %all_gather.102 = bf16[1280,320]{1,0:T(8,128)(2,1)S(1)} all-gather(bf16[160,320]{1,0:T(8,128)(2,1)S(1)} %copy-done.25), channel_id=1, replica_groups=mesh['dp'=8,'tensor'=4] {'dp'}, dimensions={0}, use_global_device_ids=true | all-gather | bytes 921600 | tf_op jit(solution)/shard_map/all_gather | solution.py:121
  397.8 12.1 %all_gather.104 = bf16[1280,320]{1,0:T(8,128)(2,1)} all-gather(bf16[160,320]{1,0:T(8,128)(2,1)S(1)} %copy-done.28), channel_id=1, replica_groups=mesh['dp'=8,'tensor'=4] {'dp'}, dimensions={0}, use_global_device_ids=true | all-gather | bytes 921600 | tf_op jit(solution)/shard_map/all_gather | solution.py:123
  430.4 13.7 %while.65 = (s32[]{:T(128)}, bf16[2,512,4,80]{1,3,2,0:T(8,128)(2,1)S(1)}, f32[2,4,512]{2,1,0:T(4,128)S(1)}, s32[]{:T(128)}, bf16[2,512,4,80]{1,3,2,0:T(8,128)(2,...) while((s32[]{:T(128)}, ...), condition=%wide.region_15.16_spmd, body=%wide.region_12.15_spmd.sunk | while | flops 696417280 | bytes 27201636 | solution.py:53
  451.0 50.1 %reduce-scatter.16.cloned.1.call-done = bf16[1,256,1280]{2,1,0:T(8,128)(2,1)} async-done(((bf16[1,1024,1280]{2,1,0:T(8,128)(2,1)}), bf16[1,256,1280]{2,1,0:T(8,128)(2,1)}) %reduce-scatter.16.cloned.1.call-update) | async-done | bytes 655376 | tf_op jit(solution)/shard_map/reduce_scatter | solution.py:165
  507.2 17.4 %collective-permute-done = bf16[1,256,1280]{2,1,0:T(8,128)(2,1)S(1)} collective-permute-done((bf16[1,256,1280]{2,1,0:T(8,128)(2,1)S(1)}, bf16[1,256,1280]{2,1,0:T(8,128)(2,1)S(1)}, u32[]{:S(2)}, u32[]{:S(2)}) %collective-permute-start) | collective-permute-done | bytes 655392 | tf_op jit(solution)/shard_map/ppermute | solution.py:16
  524.6 17.1 %collective-permute-done.1 = bf16[1,256,1280]{2,1,0:T(8,128)(2,1)} collective-permute-done((bf16[1,256,1280]{2,1,0:T(8,128)(2,1)S(1)}, bf16[1,256,1280]{2,1,0:T(8,128)(2,1)}, u32[]{:S(2)}, u32[]{:S(2)}) %collective-permute-start.1) | collective-permute-done | bytes 655392 | tf_op jit(solution)/shard_map/ppermute | solution.py:16
  541.8 27.8 %collective-permute-done.2 = bf16[1,256,1280]{2,1,0:T(8,128)(2,1)} collective-permute-done((bf16[1,256,1280]{2,1,0:T(8,128)(2,1)}, bf16[1,256,1280]{2,1,0:T(8,128)(2,1)}, u32[]{:S(2)}, u32[]{:S(2)}) %collective-permute-start.2) | collective-permute-done | bytes 655392 | tf_op jit(solution)/shard_map/ppermute | solution.py:16
  581.2 19.7 %all-gather.20.cloned.1.call-done = bf16[1,1024,1280]{2,1,0:T(8,128)(2,1)} async-done(((bf16[1,256,1280]{2,1,0:T(8,128)(2,1)}), bf16[1,1024,1280]{2,1,0:T(8,128)(2,1)}) %all-gather.20.cloned.1.call-update) | async-done | bytes 2621456 | tf_op jit(solution)/shard_map/all_gather | solution.py:179
  600.9 17.6 %fusion.74 = (f32[1024,1280]{1,0:T(8,128)}, f32[1024,1280]{1,0:T(8,128)}) fusion(f32[1280]{0:T(1024)S(1)} %convert_element_type.329, bf16[1280,1280]{1,0:T(8,128)(2,1)} %all-gather.22.cloned.1.call-done, bf16[1,1024,1280]{2,1,0:T(8,128)(2,1)} %all-gather.20.cloned.1.call-done), kind=kOutput, calls=%fused_computation.80 | convolution fusion | flops 3438018560 | bytes 16389120 | tf_op jit(solution)/shard_map/csd,df->csf/dot_general | solution.py:180
  618.5 15.1 %all-gather.24.cloned.1.call-done = bf16[1280,1280]{1,0:T(8,128)(2,1)} async-done(((bf16[160,1280]{1,0:T(8,128)(2,1)}), bf16[1280,1280]{1,0:T(8,128)(2,1)}) %all-gather.24.cloned.1.call-update) | async-done | bytes 3276816 | tf_op jit(solution)/shard_map/all_gather | solution.py:171
  633.6 11.3 %convert_reduce_fusion = (f32[1280]{0:T(1024)}, bf16[1024,1280]{1,0:T(8,128)(2,1)S(1)}) fusion(f32[1024,1280]{1,0:T(8,128)} %get-tuple-element.443, bf16[1280,1280]{1,0:T(8,128)(2,1)} %all-gather.24.cloned.1.call-done, bf16[1,2048,1280]{2,1,0:T(8,128)(2,1)} %constant_dynamic-update-slice_fusion, s32[]{:T(128)S(6)} %select_n.24, ...), kind=kOutput, calls=%fused_computation.82 | convolution fusion | flops 3377724160 | bytes 19015684 | tf_op jit(solution)/shard_map/csd,df->csf/dot_general | solution.py:265
  651.4 52.2 %reduce-scatter.18.cloned.1.call-done = bf16[1,256,1280]{2,1,0:T(8,128)(2,1)} async-done(((bf16[1,1024,1280]{2,1,0:T(8,128)(2,1)}), bf16[1,256,1280]{2,1,0:T(8,128)(2,1)}) %reduce-scatter.18.cloned.1.call-update) | async-done | bytes 655376 | tf_op jit(solution)/shard_map/reduce_scatter | solution.py:285
  730.8 35.7 %all-gather.26.cloned.1.call-done = bf16[1,1024,1280]{2,1,0:T(8,128)(2,1)} async-done(((bf16[1,256,1280]{2,1,0:T(8,128)(2,1)}), bf16[1,1024,1280]{2,1,0:T(8,128)(2,1)}) %all-gather.26.cloned.1.call-update) | async-done | bytes 2621456 | tf_op jit(solution)/shard_map/all_gather | solution.py:292
  776.2 40.1 %while.66 = (s32[]{:T(128)}, f32[1024,4,80]{0,2,1:T(8,128)S(1)}, f32[1024,4,80]{0,2,1:T(8,128)}, bf16[2,512,4,80]{1,3,2,0:T(8,128)(2,1)}, bf16[2,512,4,80]{1,3,2...) while((s32[]{:T(128)}, f32[1024,4,80]{0,2,1:T(8,128)S(1)}, ...), condition=%wide.region_24.25_spmd.clone, body=%wide.region_22.24_spmd.clone.sunk | while | flops 1711143936 | bytes 144175888 | solution.py:91
  851.1 24.1 %all-reduce.17 = (f32[320]{0:T(512)}, f32[320]{0:T(512)}, f32[1280]{0:T(1024)}) all-reduce(f32[320]{0:T(512)S(1)} %reduce_sum.247, f32[320]{0:T(512)S(1)} %reduce_sum.249, f32[1280]{0:T(1024)S(1)} %copy-done.42), channel_id=1, replica_groups=mesh['dp'=8,'tensor'=4] {'dp'}, use_global_device_ids=true, to_apply=%region_36.37 | all-reduce | flops 1920 | bytes 15360 | tf_op jit(solution)/shard_map/psum | solution.py:390
  876.8 20.3 %reduce-scatter.24.cloned.1.call-done = bf16[160,320]{1,0:T(8,128)(2,1)} async-done(((bf16[1280,320]{1,0:T(8,128)(2,1)}), bf16[160,320]{1,0:T(8,128)(2,1)}) %reduce-scatter.24.cloned.1.call-update) | async-done | bytes 102416 | tf_op jit(solution)/shard_map/reduce_scatter | solution.py:362
  898.7 37.3 %reduce-scatter.28.cloned.1.call-done = bf16[160,320]{1,0:T(8,128)(2,1)} async-done(((bf16[1280,320]{1,0:T(8,128)(2,1)}), bf16[160,320]{1,0:T(8,128)(2,1)}) %reduce-scatter.28.cloned.1.call-update) | async-done | bytes 102416 | tf_op jit(solution)/shard_map/reduce_scatter | solution.py:368
  937.7 37.5 %reduce-scatter.22.cloned.1.call-done = bf16[160,320]{1,0:T(8,128)(2,1)} async-done(((bf16[1280,320]{1,0:T(8,128)(2,1)}), bf16[160,320]{1,0:T(8,128)(2,1)}) %reduce-scatter.22.cloned.1.call-update) | async-done | bytes 102416 | tf_op jit(solution)/shard_map/reduce_scatter | solution.py:359
  976.8 52.9 %reduce-scatter.20.cloned.1.call-done = bf16[1,256,1280]{2,1,0:T(8,128)(2,1)} async-done(((bf16[1,1024,1280]{2,1,0:T(8,128)(2,1)}), bf16[1,256,1280]{2,1,0:T(8,128)(2,1)}) %reduce-scatter.20.cloned.1.call-update) | async-done | bytes 655376 | tf_op jit(solution)/shard_map/reduce_scatter | solution.py:341
  1033.1 17.7 %all-reduce.18 = (bf16[1280]{0:T(1024)(128)(2,1)S(1)}, bf16[1280]{0:T(1024)(128)(2,1)S(1)}, bf16[1280]{0:T(1024)(128)(2,1)S(1)}, bf16[1280]{0:T(1024)(128)(2,1)S...) all-reduce(f32[1280]{0:T(1024)S(1)} %get-tuple-element.352, ...), channel_id=1, replica_groups=mesh['dp'=8,'tensor'=4] {'tensor'}, use_global_device_ids=true, to_apply=%region_29.30 | all-reduce | flops 7680 | bytes 46080 | tf_op jit(solution)/shard_map/psum | solution.py:347
  1050.8 22.5 %all-reduce.19 = (bf16[1280]{0:T(1024)(128)(2,1)S(1)}, bf16[1280]{0:T(1024)(128)(2,1)S(1)}, bf16[1280]{0:T(1024)(128)(2,1)S(1)}, bf16[1280]{0:T(1024)(128)(2,1)S...) all-reduce(bf16[1280]{0:T(1024)(128)(2,1)S(1)} %get-tuple-element.4, ...), channel_id=7, replica_groups=mesh['dp'=8,'tensor'=4] {'dp'}, use_global_device_ids=true, to_apply=%region_30.31.clone | all-reduce | flops 7680 | bytes 30720
  (336 shorter events, 292.9 us)
Async XLA Ops:
  8.1 91.9 %all-gather.10.cloned.1.call-start = ((), (), s32[]{:S(2)}) async-start(), calls=%async_computation.11 | async-start | bytes 3276800 | tf_op jit(solution)/shard_map/all_gather | solution.py:132
  45.6 144.3 %reduce-scatter.12.cloned.1.call-start = ((), (), s32[]{:S(2)}) async-start(), calls=%async_computation.12 | async-start | bytes 3276800 | tf_op jit(solution)/shard_map/reduce_scatter | solution.py:165
  138.9 56.8 %all-gather.14.cloned.1.call-start = ((), (), s32[]{:S(2)}) async-start(), calls=%async_computation.14 | async-start | bytes 3686400 | tf_op jit(solution)/shard_map/all_gather | solution.py:170
  139.5 67.7 %all-gather.16.cloned.1.call-start = ((), (), s32[]{:S(2)}) async-start(), calls=%async_computation.15 | async-start | bytes 3686400 | tf_op jit(solution)/shard_map/all_gather | solution.py:171
  140.1 123.9 %all-gather.12.cloned.1.call-start = ((), (), s32[]{:S(2)}) async-start(), calls=%async_computation.13 | async-start | bytes 3276800 | tf_op jit(solution)/shard_map/all_gather | solution.py:179
  195.1 141.2 %reduce-scatter.14.cloned.1.call-start = ((), (), s32[]{:S(2)}) async-start(), calls=%async_computation.16 | async-start | bytes 3276800 | tf_op jit(solution)/shard_map/reduce_scatter | solution.py:185
  285.4 133.2 %all-gather.18.cloned.1.call-start = ((), (), s32[]{:S(2)}) async-start(), calls=%async_computation.17 | async-start | bytes 3276800 | tf_op jit(solution)/shard_map/all_gather | solution.py:132
  365.4 135.8 %reduce-scatter.16.cloned.1.call-start = ((), (), s32[]{:S(2)}) async-start(), calls=%async_computation.18 | async-start | bytes 3276800 | tf_op jit(solution)/shard_map/reduce_scatter | solution.py:165
  450.2 131.0 %all-gather.22.cloned.1.call-start = ((), (), s32[]{:S(2)}) async-start(), calls=%async_computation.20 | async-start | bytes 3686400 | tf_op jit(solution)/shard_map/all_gather | solution.py:170
  450.9 149.9 %all-gather.20.cloned.1.call-start = ((), (), s32[]{:S(2)}) async-start(), calls=%async_computation.19 | async-start | bytes 3276800 | tf_op jit(solution)/shard_map/all_gather | solution.py:179
  506.4 127.2 %all-gather.24.cloned.1.call-start = ((), (), s32[]{:S(2)}) async-start(), calls=%async_computation.21 | async-start | bytes 3686400 | tf_op jit(solution)/shard_map/all_gather | solution.py:171
  506.4 18.2 %collective-permute-start = (bf16[1,256,1280]{2,1,0:T(8,128)(2,1)S(1)}, bf16[1,256,1280]{2,1,0:T(8,128)(2,1)S(1)}, u32[]{:S(2)}, u32[]{:S(2)}) collective-permute-start(bf16[1,256,1280]{2,1,0:T(8,128)(2,1)S(1)} %copy-done.13), channel_id=1, source_target_pairs={{0,1},{1,2},{2,3},{3,0},{4,5},{5,6},{6,7},{7,4},{8,9},{9,10},{10,1... | collective-permute-start | bytes 1966088 | tf_op jit(solution)/shard_map/ppermute | solution.py:16
  524.6 17.1 %collective-permute-start.1 = (bf16[1,256,1280]{2,1,0:T(8,128)(2,1)S(1)}, bf16[1,256,1280]{2,1,0:T(8,128)(2,1)}, u32[]{:S(2)}, u32[]{:S(2)}) collective-permute-start(bf16[1,256,1280]{2,1,0:T(8,128)(2,1)S(1)} %collective-permute-done), channel_id=1, source_target_pairs={{0,1},{1,2},{2,3},{3,0},{4,5},{5,6},{6,7},{7,4},{8,9},{9,10},{10,1... | collective-permute-start | bytes 1966088 | tf_op jit(solution)/shard_map/ppermute | solution.py:16
  541.7 27.9 %collective-permute-start.2 = (bf16[1,256,1280]{2,1,0:T(8,128)(2,1)}, bf16[1,256,1280]{2,1,0:T(8,128)(2,1)}, u32[]{:S(2)}, u32[]{:S(2)}) collective-permute-start(bf16[1,256,1280]{2,1,0:T(8,128)(2,1)} %collective-permute-done.1), channel_id=1, source_target_pairs={{0,1},{1,2},{2,3},{3,0},{4,5},{5,6},{6,7},{7,4},{8,9},{9,10},{10,1... | collective-permute-start | bytes 1966088 | tf_op jit(solution)/shard_map/ppermute | solution.py:16
  541.8 161.9 %reduce-scatter.18.cloned.1.call-start = ((), (), s32[]{:S(2)}) async-start(), calls=%async_computation.22 | async-start | bytes 3276800 | tf_op jit(solution)/shard_map/reduce_scatter | solution.py:285
  651.3 115.1 %all-gather.26.cloned.1.call-start = ((), (), s32[]{:S(2)}) async-start(), calls=%async_computation.23 | async-start | bytes 3276800 | tf_op jit(solution)/shard_map/all_gather | solution.py:292
  711.8 134.0 %reduce-scatter.32.cloned.1.call-start = ((), (), s32[]{:S(2)}) async-start(), calls=%async_computation.30 | async-start | bytes 3686400 | tf_op jit(solution)/shard_map/reduce_scatter | solution.py:278
  722.5 125.2 %reduce-scatter.30.cloned.1.call-start = ((), (), s32[]{:S(2)}) async-start(), calls=%async_computation.29 | async-start | bytes 3686400 | tf_op jit(solution)/shard_map/reduce_scatter | solution.py:275
  730.5 144.6 %reduce-scatter.26.cloned.1.call-start = ((), (), s32[]{:S(2)}) async-start(), calls=%async_computation.27 | async-start | bytes 1105920 | tf_op jit(solution)/shard_map/reduce_scatter | solution.py:365
  822.9 74.2 %reduce-scatter.24.cloned.1.call-start = ((), (), s32[]{:S(2)}) async-start(), calls=%async_computation.26 | async-start | bytes 1105920 | tf_op jit(solution)/shard_map/reduce_scatter | solution.py:362
  827.7 108.4 %reduce-scatter.28.cloned.1.call-start = ((), (), s32[]{:S(2)}) async-start(), calls=%async_computation.28 | async-start | bytes 1105920 | tf_op jit(solution)/shard_map/reduce_scatter | solution.py:368
  832.1 143.1 %reduce-scatter.22.cloned.1.call-start = ((), (), s32[]{:S(2)}) async-start(), calls=%async_computation.25 | async-start | bytes 1105920 | tf_op jit(solution)/shard_map/reduce_scatter | solution.py:359
  838.5 191.2 %reduce-scatter.20.cloned.1.call-start = ((), (), s32[]{:S(2)}) async-start(), calls=%async_computation.24 | async-start | bytes 3276800 | tf_op jit(solution)/shard_map/reduce_scatter | solution.py:341
  844.8 184.8 %copy-start.30 = (f32[1280]{0:T(1024)S(1)}, f32[1280]{0:T(1024)}, u32[]{:S(2)}) copy-start(f32[1280]{0:T(1024)} %copy-done.29) | copy-start | bytes 15364
  844.8 184.8 %copy-start.32 = (f32[256]{0:T(256)S(1)}, f32[256]{0:T(256)}, u32[]{:S(2)}) copy-start(f32[256]{0:T(256)} %copy-done.31) | copy-start | bytes 3076
  844.8 186.4 %copy-start.41 = (f32[256]{0:T(256)S(1)}, f32[256]{0:T(256)}, u32[]{:S(2)}) copy-start(f32[256]{0:T(256)} %copy-done.40) | copy-start | bytes 3076
  844.9 186.4 %copy-start.39 = (f32[256]{0:T(256)S(1)}, f32[256]{0:T(256)}, u32[]{:S(2)}) copy-start(f32[256]{0:T(256)} %copy-done.38) | copy-start | bytes 3076
  844.9 188.1 %copy-start.33 = (f32[1280]{0:T(1024)S(1)}, f32[1280]{0:T(1024)}, u32[]{:S(2)}) copy-start(f32[1280]{0:T(1024)} %get-tuple-element.354) | copy-start | bytes 15364
  844.9 188.1 %copy-start.34 = (f32[1280]{0:T(1024)S(1)}, f32[1280]{0:T(1024)}, u32[]{:S(2)}) copy-start(f32[1280]{0:T(1024)} %get-tuple-element.350) | copy-start | bytes 15364
  844.9 188.1 %copy-start.35 = (f32[1280]{0:T(1024)S(1)}, f32[1280]{0:T(1024)}, u32[]{:S(2)}) copy-start(f32[1280]{0:T(1024)} %get-tuple-element.432) | copy-start | bytes 15364
  844.9 188.1 %copy-start.36 = (f32[1280]{0:T(1024)S(1)}, f32[1280]{0:T(1024)}, u32[]{:S(2)}) copy-start(f32[1280]{0:T(1024)} %get-tuple-element.440) | copy-start | bytes 15364
  844.9 230.3 %copy-start.8 = (f32[1,256,1280]{2,1,0:T(8,128)S(1)}, f32[1,256,1280]{2,1,0:T(8,128)}, u32[]{:S(2)}) copy-start(f32[1,256,1280]{2,1,0:T(8,128)} %copy-done.7) | copy-start | bytes 3932164
  (51 other events, 1680.0 us)
Sparse Core Ops, SparseCore 0:
  45.8 54.1 all-gather.9
  139.0 50.8 reduce-scatter.11
  285.5 50.8 reduce-scatter.13
  365.5 52.9 all-gather.17
  651.5 52.0 reduce-scatter.17
  711.9 54.4 all-gather.25
Sparse Core Ops, SparseCore 1:
  141.3 31.4 all-gather.13
  174.5 32.7 all-gather.15
  209.2 54.6 all-gather.11
  450.3 50.9 reduce-scatter.15
  503.1 32.2 all-gather.21
  537.5 63.3 all-gather.19
  602.6 30.9 all-gather.23
  722.6 46.4 reduce-scatter.31
  772.3 46.8 reduce-scatter.29
  823.0 34.9 reduce-scatter.25
  861.4 35.6 reduce-scatter.23
  900.4 35.6 reduce-scatter.27
  939.5 35.7 reduce-scatter.21
  977.5 52.1 reduce-scatter.19
